TPU v7x, 32 devices: a whole 2x2x4 slice. The times are simulated.
32 devices in a mesh: dp: 2 (over x), fsdp: 16 (over z, y, core).
Axes of the slice: x: 2, y: 2, z: 4, core: 2. Of those that a mesh axis runs over, the one named last changes fastest.
Arguments:
- tokens: bfloat16 [18432, 768], P(('dp', 'fsdp')), may hold values from -6 to 6
- gain_attn: bfloat16 [768], P(('dp', 'fsdp')), may hold values from 0.25 to 1.75
- w_qkv: bfloat16 [768, 2304], P(('dp', 'fsdp')), may hold values from -0.21875 to 0.21875
- w_proj: bfloat16 [768, 768], P(('dp', 'fsdp')), may hold values from -2.5 to 2.5
- gain_moe: bfloat16 [768], P(('dp', 'fsdp')), may hold values from 0.25 to 1.75
- w_router: bfloat16 [768, 8], P(('dp', 'fsdp')), may hold values from -0.15625 to 0.15625
- w_in: bfloat16 [8, 768, 3072], P('dp', 'fsdp'), may hold values from -0.21875 to 0.21875
- w_out: bfloat16 [8, 3072, 768], P('dp', 'fsdp'), may hold values from -0.875 to 0.875
- routes: int32 [18432, 2], P(('dp', 'fsdp')), may hold values from 0 to 7, as said below
- slot_ids: int32 [18432, 2], P(('dp', 'fsdp')), may hold values from 0 to 152, as said below
- cotangent: bfloat16 [18432, 768], P(('dp', 'fsdp')), may hold values from -6 to 6
Outputs:
- output: bfloat16 [18432, 768], P(('dp', 'fsdp'))
- grad_tokens: float32 [18432, 768], P(('dp', 'fsdp'))
- d_gain_attn: float32 [768], P(('dp', 'fsdp'))
- d_qkv: float32 [768, 2304], P(('dp', 'fsdp'))
- d_proj: float32 [768, 768], P(('dp', 'fsdp'))
- d_gain_moe: float32 [768], P(('dp', 'fsdp'))
- d_router: float32 [768, 8], P(('dp', 'fsdp'))
- d_in: float32 [8, 768, 3072], P('dp', 'fsdp')
- d_out: float32 [8, 3072, 768], P('dp', 'fsdp')
Inputs may be any that keep to these rules, and one draw needn't show every extreme that they name: `routes`: each row names two different experts. `slot_ids`: among the 576 patches of one device, the pairs routed to one expert hold the distinct slots 0, 1, 2, ... in some priority order; a pair beyond the 152 slots holds 152 and is dropped. On every device some expert gets more than 152 pairs.
All inputs are finite; a program needn't handle non-finite values.
Results may differ from a plain program's by a relative error of at most 0.017.
Values may be sent and summed in bfloat16 or wider, within the bound.
No kernel may reach another device: no remote copies, remote signals or barrier semaphores. Data moves between devices by JAX's collectives and lax.ppermute only.
A program may use at most 320 MiB of HBM per device.

v0:
```python
import jax
import jax.numpy as jnp
from jax import lax
from jax.sharding import PartitionSpec as P

HEADS = 12
HEAD_DIM = 64
EXPERTS = 8
SEQ = 576
CAP = 152
norm_epsilon = 1e-06


def norm_parts(values):
    centre = values - jnp.mean(values, axis=-1, keepdims=True)
    inverse = lax.rsqrt(jnp.mean(centre * centre, axis=-1, keepdims=True) + norm_epsilon)
    return (centre * inverse, inverse)


def norm_back(grad_normed, normed, inverse):
    mean_grad = jnp.mean(grad_normed, axis=-1, keepdims=True)
    mean_cross = jnp.mean(grad_normed * normed, axis=-1, keepdims=True)
    return (grad_normed - mean_grad - normed * mean_cross) * inverse


def gelu_tanh(values):
    return jax.nn.gelu(values, approximate=True)


def head_forward(operands):
    queries, keys_head, values_head = operands
    scores = jnp.einsum(
        "isd,itd->ist", queries, keys_head, preferred_element_type=jnp.float32
    ) * HEAD_DIM ** (-0.5)
    largest = jnp.max(scores, axis=-1, keepdims=True)
    powers = jnp.exp(scores - largest)
    totals = jnp.sum(powers, axis=-1, keepdims=True)
    attn_probs = (powers / totals).astype(jnp.bfloat16)
    head_out = jnp.einsum(
        "ist,itd->isd", attn_probs, values_head, preferred_element_type=jnp.float32
    )
    return (head_out.astype(jnp.bfloat16), (largest + jnp.log(totals))[..., 0])


def head_backward(operands):
    queries, keys_head, values_head, grad_head, log_total = operands
    scores = jnp.einsum(
        "isd,itd->ist", queries, keys_head, preferred_element_type=jnp.float32
    ) * HEAD_DIM ** (-0.5)
    attn_probs = jnp.exp(scores - log_total[..., None])
    grad_probs = jnp.einsum(
        "isd,itd->ist", grad_head, values_head, preferred_element_type=jnp.float32
    )
    row_terms = jnp.sum(attn_probs * grad_probs, axis=-1, keepdims=True)
    grad_scores = (attn_probs * (grad_probs - row_terms)).astype(jnp.bfloat16)
    grad_query = jnp.einsum(
        "ist,itd->isd", grad_scores, keys_head, preferred_element_type=jnp.float32
    ) * HEAD_DIM ** (-0.5)
    grad_key = jnp.einsum(
        "ist,isd->itd", grad_scores, queries, preferred_element_type=jnp.float32
    ) * HEAD_DIM ** (-0.5)
    grad_value = jnp.einsum(
        "ist,isd->itd",
        attn_probs.astype(jnp.bfloat16),
        grad_head,
        preferred_element_type=jnp.float32,
    )
    return (grad_query, grad_key, grad_value)


def expert_forward(expert_rows, w_up, w_down):
    pre_act = jnp.einsum("ecd,edf->ecf", expert_rows, w_up, preferred_element_type=jnp.float32)
    hidden = gelu_tanh(pre_act).astype(jnp.bfloat16)
    result = jnp.einsum("ecf,efd->ecd", hidden, w_down, preferred_element_type=jnp.float32).astype(
        jnp.bfloat16
    )
    return (pre_act, hidden, result)


def expert_backward(expert_rows, pre_act, hidden, grad_result, w_up, w_down):
    grad_hidden = jnp.einsum(
        "ecd,efd->ecf", grad_result, w_down, preferred_element_type=jnp.float32
    )
    ignored, pull_back = jax.vjp(gelu_tanh, pre_act)
    grad_pre = pull_back(grad_hidden)[0].astype(jnp.bfloat16)
    grad_down = jnp.einsum("ecf,ecd->efd", hidden, grad_result, preferred_element_type=jnp.float32)
    grad_up = jnp.einsum("ecd,ecf->edf", expert_rows, grad_pre, preferred_element_type=jnp.float32)
    grad_rows = jnp.einsum(
        "ecf,edf->ecd", grad_pre, w_up, preferred_element_type=jnp.float32
    ).astype(jnp.bfloat16)
    return (grad_up, grad_down, grad_rows)


def gather_dense(gain_attn, w_qkv, w_proj, gain_moe, w_router):
    return (
        lax.all_gather(gain_attn, ("dp", "fsdp"), axis=0, tiled=True),
        lax.all_gather(w_qkv, ("dp", "fsdp"), axis=0, tiled=True),
        lax.all_gather(w_proj, ("dp", "fsdp"), axis=0, tiled=True),
        lax.all_gather(gain_moe, ("dp", "fsdp"), axis=0, tiled=True),
        lax.all_gather(w_router, ("dp", "fsdp"), axis=0, tiled=True),
    )


def gather_experts(w_in, w_out):
    local_pair = (w_in, w_out)
    return (
        lax.all_gather(local_pair[0], "fsdp", axis=1, tiled=True),
        lax.all_gather(local_pair[1], "fsdp", axis=1, tiled=True),
    )


def reduce_experts(grad_up, grad_down):
    reduced = (
        lax.psum_scatter(
            grad_up.astype(jnp.bfloat16), "fsdp", scatter_dimension=1, tiled=True
        ).astype(jnp.float32),
        lax.psum_scatter(
            grad_down.astype(jnp.bfloat16), "fsdp", scatter_dimension=1, tiled=True
        ).astype(jnp.float32),
    )
    return reduced


def per_device(
    tokens, gain_attn, w_qkv, w_proj, gain_moe, w_router, w_in, w_out, routes, slot_ids, cotangent
):
    dense_full = gather_dense(gain_attn, w_qkv, w_proj, gain_moe, w_router)
    expert_weights = gather_experts(w_in, w_out)
    rows_here = tokens.shape[0]
    images = rows_here // SEQ
    residual = tokens.astype(jnp.float32)
    normed_one, inverse_one = norm_parts(residual)
    gain_one = dense_full[0].astype(jnp.float32)
    act_one = (normed_one * gain_one).astype(jnp.bfloat16)
    qkv = jnp.dot(act_one, dense_full[1], preferred_element_type=jnp.float32).astype(jnp.bfloat16)
    split_qkv = qkv.reshape(images, SEQ, 3, HEADS, HEAD_DIM).transpose(2, 3, 0, 1, 4)
    head_out, head_lse = lax.map(head_forward, (split_qkv[0], split_qkv[1], split_qkv[2]))
    attended = head_out.transpose(1, 2, 0, 3).reshape(rows_here, -1)
    resid_mid = residual + jnp.dot(attended, dense_full[2], preferred_element_type=jnp.float32)
    normed_two, inverse_two = norm_parts(resid_mid)
    gain_two = dense_full[3].astype(jnp.float32)
    act_two = (normed_two * gain_two).astype(jnp.bfloat16)
    logits = jnp.dot(act_two, dense_full[4], preferred_element_type=jnp.float32)
    router = jax.nn.softmax(logits, axis=-1)
    expert_ids = lax.broadcasted_iota(jnp.int32, (1, 1, EXPERTS), 2)
    chosen = routes[:, :, None] == expert_ids
    gate_values = jnp.sum(jnp.where(chosen, router[:, None, :], 0.0), axis=-1)
    gates_low = gate_values.astype(jnp.bfloat16)
    slot_count = EXPERTS * CAP
    columns = lax.broadcasted_iota(jnp.int32, (1, 1, slot_count), 2)
    live_pair = slot_ids < CAP
    targets = routes * CAP + slot_ids
    matches = (targets[:, :, None] == columns) & live_pair[:, :, None]
    dispatch = jnp.sum(matches.astype(jnp.bfloat16), axis=1)
    combine = jnp.sum(
        jnp.where(matches, gates_low[:, :, None], jnp.zeros((), jnp.bfloat16)), axis=1
    )
    slot_rows = (
        jnp.einsum("tx,td->xd", dispatch, act_two, preferred_element_type=jnp.float32)
        .astype(jnp.bfloat16)
        .reshape(EXPERTS, CAP, -1)
    )
    expert_rows = lax.all_to_all(slot_rows, "dp", split_axis=0, concat_axis=1, tiled=True)
    pre_act, hidden, result = expert_forward(expert_rows, expert_weights[0], expert_weights[1])
    slot_result = lax.all_to_all(result, "dp", split_axis=1, concat_axis=0, tiled=True)
    flat_result = slot_result.reshape(slot_count, -1)
    moe_sum = jnp.einsum("tx,xd->td", combine, flat_result, preferred_element_type=jnp.float32)
    output = (resid_mid + moe_sum).astype(jnp.bfloat16)
    dense_full = gather_dense(gain_attn, w_qkv, w_proj, gain_moe, w_router)
    expert_weights = gather_experts(w_in, w_out)
    grad_slots = (
        jnp.einsum("tx,td->xd", combine, cotangent, preferred_element_type=jnp.float32)
        .astype(jnp.bfloat16)
        .reshape(EXPERTS, CAP, -1)
    )
    picked = flat_result[jnp.clip(targets, 0, slot_count - 1)]
    grad_gates = jnp.where(
        live_pair,
        jnp.einsum("tkd,td->tk", picked, cotangent, preferred_element_type=jnp.float32),
        0.0,
    )
    grad_router = jnp.sum(jnp.where(chosen, grad_gates[:, :, None], 0.0), axis=1)
    grad_logits = (
        router * (grad_router - jnp.sum(router * grad_router, axis=-1, keepdims=True))
    ).astype(jnp.bfloat16)
    d_router = jnp.einsum("td,te->de", act_two, grad_logits, preferred_element_type=jnp.float32)
    grad_act_two = jnp.einsum(
        "te,de->td", grad_logits, dense_full[4], preferred_element_type=jnp.float32
    )
    grad_expert = lax.all_to_all(grad_slots, "dp", split_axis=0, concat_axis=1, tiled=True)
    grad_up, grad_down, grad_rows = expert_backward(
        expert_rows, pre_act, hidden, grad_expert, expert_weights[0], expert_weights[1]
    )
    grad_rows = lax.all_to_all(grad_rows, "dp", split_axis=1, concat_axis=0, tiled=True)
    grad_act_two = grad_act_two + jnp.einsum(
        "tx,xd->td", dispatch, grad_rows.reshape(slot_count, -1), preferred_element_type=jnp.float32
    )
    d_gain_moe = jnp.sum(grad_act_two * normed_two, axis=0)
    grad_mid = cotangent.astype(jnp.float32) + norm_back(
        grad_act_two * gain_two, normed_two, inverse_two
    )
    grad_mid_low = grad_mid.astype(jnp.bfloat16)
    d_proj = jnp.einsum("td,te->de", attended, grad_mid_low, preferred_element_type=jnp.float32)
    grad_attended = jnp.einsum(
        "te,de->td", grad_mid_low, dense_full[2], preferred_element_type=jnp.float32
    ).astype(jnp.bfloat16)
    grad_heads = grad_attended.reshape(images, SEQ, HEADS, HEAD_DIM).transpose(2, 0, 1, 3)
    grad_query, grad_key, grad_value = lax.map(
        head_backward, (split_qkv[0], split_qkv[1], split_qkv[2], grad_heads, head_lse)
    )
    grad_qkv = (
        jnp.stack([grad_query, grad_key, grad_value])
        .transpose(2, 3, 0, 1, 4)
        .reshape(rows_here, -1)
        .astype(jnp.bfloat16)
    )
    d_qkv = jnp.einsum("td,te->de", act_one, grad_qkv, preferred_element_type=jnp.float32)
    grad_act_one = jnp.einsum(
        "te,de->td", grad_qkv, dense_full[1], preferred_element_type=jnp.float32
    )
    d_gain_attn = jnp.sum(grad_act_one * normed_one, axis=0)
    grad_tokens = grad_mid + norm_back(grad_act_one * gain_one, normed_one, inverse_one)
    dense_grads = (
        lax.psum_scatter(d_gain_attn, ("dp", "fsdp"), scatter_dimension=0, tiled=True),
        lax.psum_scatter(d_qkv, ("dp", "fsdp"), scatter_dimension=0, tiled=True),
        lax.psum_scatter(d_proj, ("dp", "fsdp"), scatter_dimension=0, tiled=True),
        lax.psum_scatter(d_gain_moe, ("dp", "fsdp"), scatter_dimension=0, tiled=True),
        lax.psum_scatter(d_router, ("dp", "fsdp"), scatter_dimension=0, tiled=True),
    )
    expert_grads = reduce_experts(grad_up, grad_down)
    return (
        output,
        grad_tokens,
        dense_grads[0],
        dense_grads[1],
        dense_grads[2],
        dense_grads[3],
        dense_grads[4],
        expert_grads[0],
        expert_grads[1],
    )


def solution(mesh):
    in_specs = (
        P(("dp", "fsdp"), None),
        P(("dp", "fsdp")),
        P(("dp", "fsdp"), None),
        P(("dp", "fsdp"), None),
        P(("dp", "fsdp")),
        P(("dp", "fsdp"), None),
        P("dp", "fsdp", None),
        P("dp", "fsdp", None),
        P(("dp", "fsdp"), None),
        P(("dp", "fsdp"), None),
        P(("dp", "fsdp"), None),
    )
    out_specs = (
        P(("dp", "fsdp"), None),
        P(("dp", "fsdp"), None),
        P(("dp", "fsdp")),
        P(("dp", "fsdp"), None),
        P(("dp", "fsdp"), None),
        P(("dp", "fsdp")),
        P(("dp", "fsdp"), None),
        P("dp", "fsdp", None),
        P("dp", "fsdp", None),
    )
    return jax.shard_map(
        per_device, mesh=mesh, in_specs=in_specs, out_specs=out_specs, check_vma=False
    )
```

profile of v0, /device:TPU:0, one launch (start us, length us, event | category | flops | bytes accessed | tf_op | source)
XLA Modules:
  0.0 1001.7 jit_solution(7998535637937780949)
XLA Ops:
  10.6 42.0 %all-reduce.6 = (bf16[768]{0:T(1024)(128)(2,1)S(1)}, bf16[768]{0:T(1024)(128)(2,1)S(1)}) all-reduce(bf16[768]{0:T(1024)(128)(2,1)S(1)} %dynamic-update-slice, bf16[768]{0:T(1024)(128)(2,1)S(1)} %dynamic-update-slice.1), channel_id=1, replica_groups=mesh['dp'=2,'fsdp'=16] {'dp','fsdp'}, use_global_device_ids=true, to_apply=%add | all-reduce | flops 1536 | bytes 6144
  52.6 40.8 %all-gather = bf16[32,24,8]{1,2,0:T(8,128)(2,1)S(1)} all-gather(bf16[1,24,8]{1,2,0:T(8,128)(2,1)S(1)} %bitcast.199), channel_id=1, replica_groups=mesh['dp'=2,'fsdp'=16] {'dp','fsdp'}, dimensions={0}, use_global_device_ids=true | all-gather | bytes 12672 | tf_op jit(solution)/shard_map/all_gather | solution.py:100
  95.4 5.9 convolution_convert_fusion.3
  101.3 4.0 copy.102
  110.8 2.6 copy.105
  113.4 37.9 %while.26 = (s32[]{:T(128)}, bf16[12,1,576,64]{2,3,1,0:T(8,128)(2,1)}, f32[12,1,576]{2,1,0:T(1,128)}, bf16[12,1,576,64]{3,2,1,0:T(8,128)(2,1)S(1)}, bf16[12,1,57...) while((s32[]{:T(128)}, bf16[12,1,576,64]{2,3,1,0:T(8,128)(2,1)}, ...), condition=%wide.region_5.6_spmd, body=%wide.region_2.5_spmd.sunk | while | flops 87293376 | bytes 4531033 | solution.py:137
  114.0 1.9 fusion.134
  117.1 1.9 fusion.134
  120.3 1.9 fusion.134
  123.4 1.9 fusion.134
  126.6 1.9 fusion.134
  129.7 1.9 fusion.134
  132.8 1.9 fusion.134
  136.0 2.0 fusion.134
  139.2 1.9 fusion.134
  142.3 2.0 fusion.134
  145.5 2.0 fusion.134
  148.7 2.0 fusion.134
  151.3 4.1 fusion.75
  157.2 3.7 fusion.48
  160.9 2.9 convolution_convert_fusion.4
  163.8 3.7 all-to-all-start.2
  167.5 4.4 convolution_convert_fusion.5
  171.9 18.5 %all-to-all-done.2 = bf16[8,152,768]{2,1,0:T(8,128)(2,1)S(1)} async-done(((bf16[8,152,768]{2,1,0:T(8,128)(2,1)}), bf16[8,152,768]{2,1,0:T(8,128)(2,1)S(1)}, u32[]{:S(2)}, u32[]{:S(2)}) %all-to-all-start.2) | async-done | bytes 1867808 | tf_op jit(solution)/shard_map/all_to_all | solution.py:190
  191.7 4.8 all-to-all-start
  198.6 20.2 %all-to-all-done = bf16[8,152,768]{2,1,0:T(8,128)(2,1)} async-done(((bf16[8,152,768]{2,1,0:T(8,128)(2,1)}), bf16[8,152,768]{2,1,0:T(8,128)(2,1)}, u32[]{:S(2)}, u32[]{:S(2)}) %all-to-all-start) | async-done | bytes 1867808 | tf_op jit(solution)/shard_map/all_to_all | solution.py:163
  218.8 2.9 copy.107
  221.7 7.1 all-gather.12.cloned.1.call-done
  228.8 12.9 %fusion.77 = f32[4,304,3072]{2,1,0:T(8,128)} fusion(bf16[4,304,768]{2,1,0:T(8,128)(2,1)S(1)} %bitcast.182, bf16[4,3072,768]{2,1,0:T(8,128)(2,1)} %all-gather.12.cloned.1.call-done), kind=kOutput, calls=%fused_computation.141 | convolution fusion | flops 5737807872 | bytes 35684352 | tf_op jit(solution)/shard_map/ecd,efd->ecf/dot_general | solution.py:81
  241.7 87.4 %all-gather.10.cloned.1.call-done = bf16[4,768,3072]{2,1,0:T(8,128)(2,1)} async-done(((bf16[4,48,3072]{2,1,0:T(8,128)(2,1)}), bf16[4,768,3072]{2,1,0:T(8,128)(2,1)}) %all-gather.10.cloned.1.call-update) | async-done | bytes 18874384 | tf_op jit(solution)/shard_map/all_gather | solution.py:107
  329.1 26.9 %fusion.43 = (bf16[4,304,3072]{2,1,0:T(8,128)(2,1)}, f32[4,304,3072]{2,1,0:T(8,128)}) fusion(f32[4,304,3072]{2,1,0:T(8,128)} %fusion.77, bf16[4,304,768]{2,1,0:T(8,128)(2,1)} %bitcast.192, bf16[4,768,3072]{2,1,0:T(8,128)(2,1)} %all-gather.10.cloned.1.call-done), kind=kOutput, calls=%fused_computation.59 | convolution fusion | flops 5812518912 | bytes 58097664 | tf_op jit(solution)/shard_map/ecd,edf->ecf/dot_general | solution.py:72
  356.0 16.5 %convolution_convert_fusion.2 = bf16[4,768,3072]{2,1,0:T(8,128)(2,1)} fusion(bf16[4,304,768]{2,1,0:T(8,128)(2,1)} %bitcast.193, bf16[4,304,3072]{2,1,0:T(8,128)(2,1)} %get-tuple-element.212), kind=kOutput, calls=%fused_computation.62 | convolution fusion | flops 5747245056 | bytes 28213248 | tf_op jit(solution)/shard_map/ecd,ecf->edf/dot_general | solution.py:87
  372.8 20.0 %convolution_convert_fusion.1 = bf16[4,3072,768]{2,1,0:T(8,128)(2,1)} fusion(bf16[4,304,768]{2,1,0:T(8,128)(2,1)S(1)} %bitcast.183, f32[4,304,3072]{2,1,0:T(8,128)} %get-tuple-element.213), kind=kOutput, calls=%fused_computation.61 | convolution fusion | flops 5780865024 | bytes 35684352 | tf_op jit(solution)/shard_map/ecf,ecd->efd/dot_general | solution.py:86
  392.9 19.3 %convolution_convert_fusion.7 = bf16[4,304,768]{2,1,0:T(8,128)(2,1)S(1)} fusion(bf16[4,3072,768]{2,1,0:T(8,128)(2,1)} %all-gather.12.cloned.1.call-done, f32[4,304,3072]{2,1,0:T(8,128)} %get-tuple-element.213), kind=kOutput, calls=%fused_computation.85 | convolution fusion | flops 5772361728 | bytes 35684352 | tf_op jit(solution)/shard_map/ecf,efd->ecd/dot_general | solution.py:74
  412.2 2.2 copy.108
  414.4 3.9 all-to-all-start.1
  418.4 13.2 %convolution_convert_fusion.6 = bf16[4,304,768]{2,1,0:T(8,128)(2,1)} fusion(bf16[4,304,3072]{2,1,0:T(8,128)(2,1)} %get-tuple-element.212, bf16[4,768,3072]{2,1,0:T(8,128)(2,1)} %all-gather.10.cloned.1.call-done), kind=kOutput, calls=%fused_computation.84 | convolution fusion | flops 5738741760 | bytes 28213248 | tf_op jit(solution)/shard_map/ecf,edf->ecd/dot_general | solution.py:88
  431.6 3.7 copy.112
  435.3 6.1 all-to-all-done.1
  442.6 4.8 all-to-all-start.3
  449.7 20.1 %all-to-all-done.3 = bf16[4,304,768]{2,0,1:T(4,128)(2,1)} async-done(((bf16[4,304,768]{2,0,1:T(4,128)(2,1)}), bf16[4,304,768]{2,0,1:T(4,128)(2,1)}, u32[]{:S(2)}, u32[]{:S(2)}) %all-to-all-start.3) | async-done | bytes 1867808 | tf_op jit(solution)/shard_map/all_to_all | solution.py:194
  472.9 4.8 gather_fusion
  477.7 4.7 reshape.217
  482.4 6.0 fusion.62
  489.7 3.0 fusion.78
  499.1 4.3 fusion.66
  503.7 100.7 %while.27 = (s32[]{:T(128)}, bf16[12,1,576,64]{2,3,1,0:T(8,128)(2,1)}, bf16[12,1,576,64]{2,3,1,0:T(8,128)(2,1)}, bf16[12,1,576,64]{2,3,1,0:T(8,128)(2,1)}, bf16[...) while((s32[]{:T(128)}, ...), condition=%wide.region_19.20_spmd, body=%wide.region_17.19_spmd.sunk | while | flops 215064000 | bytes 11510129 | solution.py:208
  524.0 1.9 fusion.144
  534.2 1.9 fusion.145
  550.9 1.9 fusion.145
  575.9 1.9 fusion.145
  584.4 2.0 fusion.145
  593.0 1.9 fusion.145
  601.5 1.9 fusion.145
  608.4 5.5 fusion.71
  615.2 7.2 fusion.60
  622.4 43.2 %all-reduce.5 = (f32[768]{0:T(1024)S(1)}, f32[768]{0:T(1024)S(1)}, f32[768,8]{0,1:T(8,128)S(1)}) all-reduce(f32[768]{0:T(1024)S(1)} %get-tuple-element.158, f32[768]{0:T(1024)S(1)} %get-tuple-element.156, f32[768,8]{0,1:T(8,128)S(1)} %fusion.79), channel_id=2, replica_groups=mesh['dp'=2,'fsdp'=16] {'dp','fsdp'}, use_global_device_ids=true, to_apply=%region_23.24.clone | all-reduce | flops 7680 | bytes 61440
  667.4 4.0 fusion.59
  671.4 2.2 add_convert_fusion
  673.7 3.0 convert_element_type.122
  676.7 88.2 %reduce-scatter.12.cloned.1.call-done = bf16[4,192,768]{2,1,0:T(8,128)(2,1)} async-done(((bf16[4,3072,768]{2,1,0:T(8,128)(2,1)}), bf16[4,192,768]{2,1,0:T(8,128)(2,1)}) %reduce-scatter.12.cloned.1.call-update) | async-done | bytes 1179664 | tf_op jit(solution)/shard_map/reduce_scatter | solution.py:117
  764.9 2.9 convert_element_type.124
  767.8 101.8 %reduce-scatter.8.cloned.1.call-done = f32[24,768]{1,0:T(8,128)} async-done(((f32[768,768]{1,0:T(8,128)}), f32[24,768]{1,0:T(8,128)}) %reduce-scatter.8.cloned.1.call-update) | async-done | bytes 73744 | tf_op jit(solution)/shard_map/reduce_scatter | solution.py:226
  869.6 124.8 %reduce-scatter.6.cloned.1.call-done = f32[24,2304]{1,0:T(8,128)} async-done(((f32[768,2304]{1,0:T(8,128)}), f32[24,2304]{1,0:T(8,128)}) %reduce-scatter.6.cloned.1.call-update) | async-done | bytes 221200 | tf_op jit(solution)/shard_map/reduce_scatter | solution.py:225
  (276 shorter events, 138.9 us)
Async XLA Ops:
  7.2 2.9 copy-start.36
  7.2 3.1 copy-start.37
  7.2 45.4 %copy-start.34 = (bf16[24,8]{0,1:T(8,128)(2,1)S(1)}, bf16[24,8]{0,1:T(8,128)(2,1)}, u32[]{:S(2)}) copy-start(bf16[24,8]{0,1:T(8,128)(2,1)} %param.20) | copy-start | bytes 1156
  7.2 86.3 %copy-start.8 = (bf16[576,768]{1,0:T(8,128)(2,1)S(1)}, bf16[576,768]{1,0:T(8,128)(2,1)}, u32[]{:S(2)}) copy-start(bf16[576,768]{1,0:T(8,128)(2,1)} %param.15) | copy-start | bytes 2654212
  7.2 88.2 %all-gather.6.cloned.1.call-start = ((), (), s32[]{:S(2)}) async-start(), calls=%async_computation.8 | async-start | bytes 3649536 | tf_op jit(solution)/shard_map/all_gather | solution.py:97
  8.0 143.4 %all-gather.8.cloned.1.call-start = ((), (), s32[]{:S(2)}) async-start(), calls=%async_computation.9 | async-start | bytes 1216512 | tf_op jit(solution)/shard_map/all_gather | solution.py:98
  8.7 220.1 %all-gather.12.cloned.1.call-start = ((), (), s32[]{:S(2)}) async-start(), calls=%async_computation.11 | async-start | bytes 20054016 | tf_op jit(solution)/shard_map/all_gather | solution.py:108
  9.4 84.7 %copy-start.21 = (s32[576,2]{0,1:T(2,128)S(1)}, s32[576,2]{0,1:T(2,128)}, u32[]{:S(2)}) copy-start(s32[576,2]{0,1:T(2,128)} %param.24) | copy-start | bytes 13828
  9.4 85.3 %copy-start.23 = (s32[576,2]{0,1:T(2,128)S(1)}, s32[576,2]{0,1:T(2,128)}, u32[]{:S(2)}) copy-start(s32[576,2]{0,1:T(2,128)} %param.23) | copy-start | bytes 13828
  9.5 319.6 %all-gather.10.cloned.1.call-start = ((), (), s32[]{:S(2)}) async-start(), calls=%async_computation.10 | async-start | bytes 20054016 | tf_op jit(solution)/shard_map/all_gather | solution.py:107
  52.6 42.8 %copy-start.29 = (f32[768]{0:T(1024)}, f32[768]{0:T(1024)S(1)}, u32[]{:S(2)}) copy-start(f32[768]{0:T(1024)S(1)} %convert_element_type.101) | copy-start | bytes 9220
  93.7 1.6 copy-start.25
  94.8 0.6 copy-start.31
  151.3 4.1 copy-start.4
  151.3 4.2 copy-start.5
  155.5 1.2 copy-start
  155.9 1.2 copy-start.24
  155.9 1.3 copy-start.27
  155.9 1.3 copy-start.33
  156.7 10.9 %copy-start.6 = (bf16[576,768]{1,0:T(8,128)(2,1)}, bf16[576,768]{1,0:T(8,128)(2,1)S(1)}, u32[]{:S(2)}) copy-start(bf16[576,768]{1,0:T(8,128)(2,1)S(1)} %multiply_convert_fusion.2) | copy-start | bytes 2654212
  156.7 4.2 copy-start.19
  160.9 2.9 copy-start.14
  163.8 26.7 %all-to-all-start.2 = ((bf16[8,152,768]{2,1,0:T(8,128)(2,1)}), bf16[8,152,768]{2,1,0:T(8,128)(2,1)S(1)}, u32[]{:S(2)}, u32[]{:S(2)}) async-start(bf16[8,152,768]{2,1,0:T(8,128)(2,1)} %bitcast.194), calls=%async_computation.2 | async-start | bytes 3735552 | tf_op jit(solution)/shard_map/all_to_all | solution.py:190
  190.5 1.2 copy-start.12
  191.7 27.1 %all-to-all-start = ((bf16[8,152,768]{2,1,0:T(8,128)(2,1)}), bf16[8,152,768]{2,1,0:T(8,128)(2,1)}, u32[]{:S(2)}, u32[]{:S(2)}) async-start(bf16[8,152,768]{2,1,0:T(8,128)(2,1)} %bitcast.191), calls=%async_computation | async-start | bytes 3735552 | tf_op jit(solution)/shard_map/all_to_all | solution.py:163
  196.5 477.2 %reduce-scatter.10.cloned.1.call-start = ((), (), s32[]{:S(2)}) async-start(), calls=%async_computation.14 | async-start | bytes 20054016 | tf_op jit(solution)/shard_map/reduce_scatter | solution.py:114
  372.6 392.4 %reduce-scatter.12.cloned.1.call-start = ((), (), s32[]{:S(2)}) async-start(), calls=%async_computation.15 | async-start | bytes 20054016 | tf_op jit(solution)/shard_map/reduce_scatter | solution.py:117
  414.4 27.0 %all-to-all-start.1 = ((bf16[4,304,768]{2,0,1:T(4,128)(2,1)}), bf16[4,304,768]{2,0,1:T(4,128)(2,1)S(1)}, u32[]{:S(2)}, u32[]{:S(2)}) async-start(bf16[4,304,768]{2,0,1:T(4,128)(2,1)} %copy.108), calls=%async_computation.1 | async-start | bytes 3735552 | tf_op jit(solution)/shard_map/all_to_all | solution.py:165
  435.3 12.2 %copy-start.28 = (s32[576,2]{0,1:T(2,128)S(1)}, s32[576,2]{0,1:T(2,128)}, u32[]{:S(2)}) copy-start(s32[576,2]{0,1:T(2,128)} %get-tuple-element.199) | copy-start | bytes 13828
  441.4 1.2 copy-start.11
  442.6 27.1 %all-to-all-start.3 = ((bf16[4,304,768]{2,0,1:T(4,128)(2,1)}), bf16[4,304,768]{2,0,1:T(4,128)(2,1)}, u32[]{:S(2)}, u32[]{:S(2)}) async-start(bf16[4,304,768]{2,0,1:T(4,128)(2,1)} %copy.112), calls=%async_computation.3 | async-start | bytes 3735552 | tf_op jit(solution)/shard_map/all_to_all | solution.py:194
  447.4 422.2 %reduce-scatter.8.cloned.1.call-start = ((), (), s32[]{:S(2)}) async-start(), calls=%async_computation.13 | async-start | bytes 2433024 | tf_op jit(solution)/shard_map/reduce_scatter | solution.py:226
  482.4 7.1 copy-start.22
  482.4 7.3 copy-start.16
  489.7 3.0 copy-start.1
  492.7 1.2 copy-start.20
  493.8 1.9 copy-start.35
  494.5 1.2 copy-start.3
  503.4 491.0 %reduce-scatter.6.cloned.1.call-start = ((), (), s32[]{:S(2)}) async-start(), calls=%async_computation.12 | async-start | bytes 7299072 | tf_op jit(solution)/shard_map/reduce_scatter | solution.py:225
  604.4 1.5 copy-start.17
  604.4 1.8 copy-start.18
  606.1 2.2 copy-start.9
  606.2 2.2 copy-start.26
  606.2 2.2 copy-start.30
  606.2 2.2 copy-start.32
  606.7 1.7 copy-start.13
  613.8 1.2 copy-start.7
  615.2 52.2 %copy-start.10 = (bf16[576,768]{1,0:T(8,128)(2,1)S(1)}, bf16[576,768]{1,0:T(8,128)(2,1)}, u32[]{:S(2)}) copy-start(bf16[576,768]{1,0:T(8,128)(2,1)} %param.15) | copy-start | bytes 2654212
  667.4 4.0 copy-start.2
  667.4 4.0 copy-start.15
Sparse Core Ops, SparseCore 0:
  10.9 62.6 all-gather.5
  76.6 52.6 all-gather.7
  130.9 97.8 all-gather.11
  230.2 98.8 all-gather.9
  372.7 194.0 reduce-scatter.9
  570.7 194.1 reduce-scatter.11
  770.8 98.7 reduce-scatter.7
  875.8 118.5 reduce-scatter.5
where the time goes:
time: 1010 us; the launch traced here: 1000 us
  waiting for transfers between devices  477 us (47%)
  matrix products  276 us (27%)
  blocking collectives  126 us (12%)
  local copies, waits for them, and re-layouts  66.9 us (7%)
  other arithmetic  22.4 us (2%)
  starting transfers between devices  18.3 us (2%)
  between operations  15.1 us (1%)
    reduce_scatter x1, waiting for transfers between devices, per_device(): lax.psum_scatter(d_qkv, ('dp', 'fsdp'), scatter_dimension=0, tiled=True)  125 us
    reduce_scatter x1, waiting for transfers between devices, per_device(): lax.psum_scatter(d_proj, ('dp', 'fsdp'), scatter_dimension=0, tiled=True)  102 us
    reduce_scatter x1, waiting for transfers between devices, reduce_experts(): lax.psum_scatter(grad_down.astype(jnp.bfloat16), 'fsdp', scatter_dimensio...  88.2 us
    all_gather x1, waiting for transfers between devices, gather_experts(): lax.all_gather(local_pair[0], 'fsdp', axis=1, tiled=True)  87.4 us
    unnamed x2, blocking collectives  85.2 us
    all_gather x1, blocking collectives, gather_dense(): lax.all_gather(w_router, ('dp', 'fsdp'), axis=0, tiled=True)  40.8 us
    dot_general x1, matrix products, expert_forward(): jnp.einsum('ecd,edf->ecf', expert_rows, w_up, preferred_element_type=jnp....  26.9 us
    dot_general x12, matrix products, head_forward(): jnp.einsum('ist,itd->isd', attn_probs, values_head, preferred_element_typ...  23.4 us
  transfers between devices with their start and end apart: 12, of which 9 were waited for; matrix products, arithmetic and copies ran while one was open for 31% of the time, Pallas kernels for 0%

commit v1 on v0

--- a/solution.py
+++ b/solution.py
@@ -191,7 +191,10 @@
     grad_up, grad_down, grad_rows = expert_backward(
         expert_rows, pre_act, hidden, grad_expert, expert_weights[0], expert_weights[1]
     )
-    grad_rows = lax.all_to_all(grad_rows, "dp", split_axis=1, concat_axis=0, tiled=True)
+    grad_rows = jnp.concatenate(
+        lax.all_to_all(jnp.stack(jnp.split(grad_rows, lax.axis_size("dp"), axis=1), 0), "dp", 0, 0),
+        0,
+    )
     grad_act_two = grad_act_two + jnp.einsum(
         "tx,xd->td", dispatch, grad_rows.reshape(slot_count, -1), preferred_element_type=jnp.float32
     )

time: 1010 us -> 1010 us (level)
    reduce_scatter x1, waiting for transfers between devices: 88.2 us -> 106 us  [reduce_experts(): lax.psum_scatter(grad_down.astype(jnp.bfloat16), 'fsdp', scatter_dimensio...]
    all_to_all x1, waiting for transfers between devices: 20.1 us -> 3.86 us  [per_device(): lax.all_to_all(jnp.stack(jnp.split(grad_rows, lax.axis_size('dp'), axis=1...]
where the time goes in v1:
time: 1010 us; the launch traced here: 1000 us
  waiting for transfers between devices  479 us (47%)
  matrix products  275 us (27%)
  blocking collectives  127 us (13%)
  local copies, waits for them, and re-layouts  63 us (6%)
  other arithmetic  23.7 us (2%)
  starting transfers between devices  18.3 us (2%)
  between operations  15.1 us (1%)
    reduce_scatter x1, waiting for transfers between devices, per_device(): lax.psum_scatter(d_qkv, ('dp', 'fsdp'), scatter_dimension=0, tiled=True)  125 us
    reduce_scatter x1, waiting for transfers between devices, reduce_experts(): lax.psum_scatter(grad_down.astype(jnp.bfloat16), 'fsdp', scatter_dimensio...  106 us
    reduce_scatter x1, waiting for transfers between devices, per_device(): lax.psum_scatter(d_proj, ('dp', 'fsdp'), scatter_dimension=0, tiled=True)  102 us
    all_gather x1, waiting for transfers between devices, gather_experts(): lax.all_gather(local_pair[0], 'fsdp', axis=1, tiled=True)  87.4 us
    unnamed x2, blocking collectives  86.2 us
    all_gather x1, blocking collectives, gather_dense(): lax.all_gather(w_router, ('dp', 'fsdp'), axis=0, tiled=True)  40.8 us
    dot_general x1, matrix products, expert_forward(): jnp.einsum('ecd,edf->ecf', expert_rows, w_up, preferred_element_type=jnp....  26.7 us
    dot_general x12, matrix products, head_forward(): jnp.einsum('ist,itd->isd', attn_probs, values_head, preferred_element_typ...  23.4 us
  transfers between devices with their start and end apart: 12, of which 9 were waited for; matrix products, arithmetic and copies ran while one was open for 31% of the time, Pallas kernels for 0%

profile of v1, /device:TPU:0, one launch (start us, length us, event | category | flops | bytes accessed | tf_op | source)
XLA Modules:
  0.0 1001.5 jit_solution(12770171559320895816)
XLA Ops:
  10.6 42.0 %all-reduce.6 = (bf16[768]{0:T(1024)(128)(2,1)S(1)}, bf16[768]{0:T(1024)(128)(2,1)S(1)}) all-reduce(bf16[768]{0:T(1024)(128)(2,1)S(1)} %dynamic-update-slice, bf16[768]{0:T(1024)(128)(2,1)S(1)} %dynamic-update-slice.1), channel_id=1, replica_groups=mesh['dp'=2,'fsdp'=16] {'dp','fsdp'}, use_global_device_ids=true, to_apply=%add | all-reduce | flops 1536 | bytes 6144
  52.6 40.8 %all-gather = bf16[32,24,8]{1,2,0:T(8,128)(2,1)S(1)} all-gather(bf16[1,24,8]{1,2,0:T(8,128)(2,1)S(1)} %bitcast.198), channel_id=1, replica_groups=mesh['dp'=2,'fsdp'=16] {'dp','fsdp'}, dimensions={0}, use_global_device_ids=true | all-gather | bytes 12672 | tf_op jit(solution)/shard_map/all_gather | solution.py:100
  95.4 5.9 convolution_convert_fusion.3
  101.2 4.0 copy.75
  110.8 2.6 copy.78
  113.3 37.9 %while.26 = (s32[]{:T(128)}, bf16[12,1,576,64]{2,3,1,0:T(8,128)(2,1)}, f32[12,1,576]{2,1,0:T(1,128)}, bf16[12,1,576,64]{3,2,1,0:T(8,128)(2,1)S(1)}, bf16[12,1,57...) while((s32[]{:T(128)}, bf16[12,1,576,64]{2,3,1,0:T(8,128)(2,1)}, ...), condition=%wide.region_5.6_spmd, body=%wide.region_2.5_spmd.sunk | while | flops 87293376 | bytes 4531033 | solution.py:137
  114.0 1.9 fusion.134
  117.1 1.9 fusion.134
  120.2 1.9 fusion.134
  123.4 1.9 fusion.134
  126.5 1.9 fusion.134
  129.7 1.9 fusion.134
  132.8 1.9 fusion.134
  136.0 2.0 fusion.134
  139.2 1.9 fusion.134
  142.3 2.0 fusion.134
  145.5 2.0 fusion.134
  148.7 2.0 fusion.134
  151.3 4.1 fusion.75
  157.1 3.7 fusion.48
  160.8 2.9 convolution_convert_fusion.4
  163.7 3.7 all-to-all-start.2
  167.5 4.4 convolution_convert_fusion.5
  171.9 18.5 %all-to-all-done.2 = bf16[8,152,768]{2,1,0:T(8,128)(2,1)S(1)} async-done(((bf16[8,152,768]{2,1,0:T(8,128)(2,1)}), bf16[8,152,768]{2,1,0:T(8,128)(2,1)S(1)}, u32[]{:S(2)}, u32[]{:S(2)}) %all-to-all-start.2) | async-done | bytes 1867808 | tf_op jit(solution)/shard_map/all_to_all | solution.py:190
  191.7 4.8 all-to-all-start
  198.6 20.2 %all-to-all-done = bf16[8,152,768]{2,1,0:T(8,128)(2,1)} async-done(((bf16[8,152,768]{2,1,0:T(8,128)(2,1)}), bf16[8,152,768]{2,1,0:T(8,128)(2,1)}, u32[]{:S(2)}, u32[]{:S(2)}) %all-to-all-start) | async-done | bytes 1867808 | tf_op jit(solution)/shard_map/all_to_all | solution.py:163
  218.8 2.9 copy.80
  221.7 7.1 all-gather.12.cloned.1.call-done
  228.8 12.9 %fusion.77 = f32[4,304,3072]{2,1,0:T(8,128)} fusion(bf16[4,304,768]{2,1,0:T(8,128)(2,1)S(1)} %bitcast.183, bf16[4,3072,768]{2,1,0:T(8,128)(2,1)} %all-gather.12.cloned.1.call-done), kind=kOutput, calls=%fused_computation.144 | convolution fusion | flops 5737807872 | bytes 35684352 | tf_op jit(solution)/shard_map/ecd,efd->ecf/dot_general | solution.py:81
  241.7 87.4 %all-gather.10.cloned.1.call-done = bf16[4,768,3072]{2,1,0:T(8,128)(2,1)} async-done(((bf16[4,48,3072]{2,1,0:T(8,128)(2,1)}), bf16[4,768,3072]{2,1,0:T(8,128)(2,1)}) %all-gather.10.cloned.1.call-update) | async-done | bytes 18874384 | tf_op jit(solution)/shard_map/all_gather | solution.py:107
  329.1 26.7 %fusion.43 = (bf16[4,304,3072]{2,1,0:T(8,128)(2,1)}, f32[4,304,3072]{2,1,0:T(8,128)}) fusion(f32[4,304,3072]{2,1,0:T(8,128)} %fusion.77, bf16[4,304,768]{2,1,0:T(8,128)(2,1)} %bitcast.191, bf16[4,768,3072]{2,1,0:T(8,128)(2,1)} %all-gather.10.cloned.1.call-done), kind=kOutput, calls=%fused_computation.59 | convolution fusion | flops 5812518912 | bytes 58097664 | tf_op jit(solution)/shard_map/ecd,edf->ecf/dot_general | solution.py:72
  355.8 16.5 %convolution_convert_fusion.2 = bf16[4,768,3072]{2,1,0:T(8,128)(2,1)} fusion(bf16[4,304,768]{2,1,0:T(8,128)(2,1)} %bitcast.192, bf16[4,304,3072]{2,1,0:T(8,128)(2,1)} %get-tuple-element.199), kind=kOutput, calls=%fused_computation.62 | convolution fusion | flops 5747245056 | bytes 28213248 | tf_op jit(solution)/shard_map/ecd,ecf->edf/dot_general | solution.py:87
  372.5 20.0 %convolution_convert_fusion.1 = bf16[4,3072,768]{2,1,0:T(8,128)(2,1)} fusion(bf16[4,304,768]{2,1,0:T(8,128)(2,1)S(1)} %bitcast.184, f32[4,304,3072]{2,1,0:T(8,128)} %get-tuple-element.200), kind=kOutput, calls=%fused_computation.61 | convolution fusion | flops 5780865024 | bytes 35684352 | tf_op jit(solution)/shard_map/ecf,ecd->efd/dot_general | solution.py:86
  393.7 18.9 %convolution_convert_fusion.7 = bf16[4,304,768]{2,1,0:T(8,128)(2,1)S(1)} fusion(bf16[4,3072,768]{2,1,0:T(8,128)(2,1)} %all-gather.12.cloned.1.call-done, f32[4,304,3072]{2,1,0:T(8,128)} %get-tuple-element.200), kind=kOutput, calls=%fused_computation.86 | convolution fusion | flops 5772361728 | bytes 35684352 | tf_op jit(solution)/shard_map/ecf,efd->ecd/dot_general | solution.py:74
  412.5 2.2 copy.81
  414.7 3.9 all-to-all-start.1
  418.7 13.2 %convolution_convert_fusion.6 = bf16[4,304,768]{2,1,0:T(8,128)(2,1)} fusion(bf16[4,304,3072]{2,1,0:T(8,128)(2,1)} %get-tuple-element.199, bf16[4,768,3072]{2,1,0:T(8,128)(2,1)} %all-gather.10.cloned.1.call-done), kind=kOutput, calls=%fused_computation.85 | convolution fusion | flops 5738741760 | bytes 28213248 | tf_op jit(solution)/shard_map/ecf,edf->ecd/dot_general | solution.py:88
  434.9 6.8 all-to-all-done.1
  443.0 4.7 all-to-all-start.3
  449.5 4.8 gather_fusion
  454.3 4.7 reshape.212
  459.0 6.0 fusion.62
  466.2 3.9 all-to-all-done.3
  470.1 3.0 fusion.78
  479.4 4.3 fusion.66
  484.0 100.3 %while.27 = (s32[]{:T(128)}, bf16[12,1,576,64]{2,3,1,0:T(8,128)(2,1)}, bf16[12,1,576,64]{2,3,1,0:T(8,128)(2,1)}, bf16[12,1,576,64]{2,3,1,0:T(8,128)(2,1)}, bf16[...) while((s32[]{:T(128)}, ...), condition=%wide.region_19.20_spmd, body=%wide.region_17.19_spmd.sunk | while | flops 215064000 | bytes 11510129 | solution.py:211
  506.2 1.9 fusion.145
  514.5 1.9 fusion.145
  522.8 1.9 fusion.145
  547.8 1.9 fusion.145
  556.2 1.9 fusion.145
  564.5 1.9 fusion.145
  572.9 1.9 fusion.145
  581.4 1.9 fusion.145
  588.9 5.8 fusion.71
  596.2 7.8 fusion.60
  604.0 44.1 %all-reduce.5 = (f32[768]{0:T(1024)S(1)}, f32[768]{0:T(1024)S(1)}, f32[768,8]{0,1:T(8,128)S(1)}) all-reduce(f32[768]{0:T(1024)S(1)} %get-tuple-element.143, f32[768]{0:T(1024)S(1)} %get-tuple-element.141, f32[768,8]{0,1:T(8,128)S(1)} %fusion.79), channel_id=2, replica_groups=mesh['dp'=2,'fsdp'=16] {'dp','fsdp'}, use_global_device_ids=true, to_apply=%region_23.24.clone | all-reduce | flops 7680 | bytes 61440
  650.0 4.0 fusion.59
  654.0 2.2 add_convert_fusion
  656.2 2.9 convert_element_type.122
  659.2 105.6 %reduce-scatter.12.cloned.1.call-done = bf16[4,192,768]{2,1,0:T(8,128)(2,1)} async-done(((bf16[4,3072,768]{2,1,0:T(8,128)(2,1)}), bf16[4,192,768]{2,1,0:T(8,128)(2,1)}) %reduce-scatter.12.cloned.1.call-update) | async-done | bytes 1179664 | tf_op jit(solution)/shard_map/reduce_scatter | solution.py:117
  764.7 2.9 convert_element_type.124
  767.6 101.7 %reduce-scatter.8.cloned.1.call-done = f32[24,768]{1,0:T(8,128)} async-done(((f32[768,768]{1,0:T(8,128)}), f32[24,768]{1,0:T(8,128)}) %reduce-scatter.8.cloned.1.call-update) | async-done | bytes 73744 | tf_op jit(solution)/shard_map/reduce_scatter | solution.py:229
  869.3 125.0 %reduce-scatter.6.cloned.1.call-done = f32[24,2304]{1,0:T(8,128)} async-done(((f32[768,2304]{1,0:T(8,128)}), f32[24,2304]{1,0:T(8,128)}) %reduce-scatter.6.cloned.1.call-update) | async-done | bytes 221200 | tf_op jit(solution)/shard_map/reduce_scatter | solution.py:228
  (275 shorter events, 137.8 us)
Async XLA Ops:
  7.2 2.9 copy-start.36
  7.2 3.1 copy-start.37
  7.2 45.4 %copy-start.34 = (bf16[24,8]{0,1:T(8,128)(2,1)S(1)}, bf16[24,8]{0,1:T(8,128)(2,1)}, u32[]{:S(2)}) copy-start(bf16[24,8]{0,1:T(8,128)(2,1)} %param.20) | copy-start | bytes 1156
  7.2 86.3 %copy-start.8 = (bf16[576,768]{1,0:T(8,128)(2,1)S(1)}, bf16[576,768]{1,0:T(8,128)(2,1)}, u32[]{:S(2)}) copy-start(bf16[576,768]{1,0:T(8,128)(2,1)} %param.15) | copy-start | bytes 2654212
  7.2 88.2 %all-gather.6.cloned.1.call-start = ((), (), s32[]{:S(2)}) async-start(), calls=%async_computation.8 | async-start | bytes 3649536 | tf_op jit(solution)/shard_map/all_gather | solution.py:97
  8.0 143.3 %all-gather.8.cloned.1.call-start = ((), (), s32[]{:S(2)}) async-start(), calls=%async_computation.9 | async-start | bytes 1216512 | tf_op jit(solution)/shard_map/all_gather | solution.py:98
  8.7 220.1 %all-gather.12.cloned.1.call-start = ((), (), s32[]{:S(2)}) async-start(), calls=%async_computation.11 | async-start | bytes 20054016 | tf_op jit(solution)/shard_map/all_gather | solution.py:108
  9.4 84.7 %copy-start.21 = (s32[576,2]{0,1:T(2,128)S(1)}, s32[576,2]{0,1:T(2,128)}, u32[]{:S(2)}) copy-start(s32[576,2]{0,1:T(2,128)} %param.24) | copy-start | bytes 13828
  9.4 85.3 %copy-start.23 = (s32[576,2]{0,1:T(2,128)S(1)}, s32[576,2]{0,1:T(2,128)}, u32[]{:S(2)}) copy-start(s32[576,2]{0,1:T(2,128)} %param.23) | copy-start | bytes 13828
  9.5 319.6 %all-gather.10.cloned.1.call-start = ((), (), s32[]{:S(2)}) async-start(), calls=%async_computation.10 | async-start | bytes 20054016 | tf_op jit(solution)/shard_map/all_gather | solution.py:107
  52.6 42.8 %copy-start.29 = (f32[768]{0:T(1024)}, f32[768]{0:T(1024)S(1)}, u32[]{:S(2)}) copy-start(f32[768]{0:T(1024)S(1)} %convert_element_type.101) | copy-start | bytes 9220
  93.7 1.6 copy-start.25
  94.8 0.6 copy-start.31
  151.3 4.1 copy-start.4
  151.3 4.1 copy-start.5
  155.4 1.2 copy-start
  155.8 1.2 copy-start.24
  155.8 1.3 copy-start.27
  155.8 1.3 copy-start.33
  156.6 10.9 %copy-start.6 = (bf16[576,768]{1,0:T(8,128)(2,1)}, bf16[576,768]{1,0:T(8,128)(2,1)S(1)}, u32[]{:S(2)}) copy-start(bf16[576,768]{1,0:T(8,128)(2,1)S(1)} %multiply_convert_fusion.2) | copy-start | bytes 2654212
  156.6 4.2 copy-start.19
  160.8 2.9 copy-start.14
  163.7 26.7 %all-to-all-start.2 = ((bf16[8,152,768]{2,1,0:T(8,128)(2,1)}), bf16[8,152,768]{2,1,0:T(8,128)(2,1)S(1)}, u32[]{:S(2)}, u32[]{:S(2)}) async-start(bf16[8,152,768]{2,1,0:T(8,128)(2,1)} %bitcast.193), calls=%async_computation.2 | async-start | bytes 3735552 | tf_op jit(solution)/shard_map/all_to_all | solution.py:190
  190.4 1.2 copy-start.12
  191.7 27.1 %all-to-all-start = ((bf16[8,152,768]{2,1,0:T(8,128)(2,1)}), bf16[8,152,768]{2,1,0:T(8,128)(2,1)}, u32[]{:S(2)}, u32[]{:S(2)}) async-start(bf16[8,152,768]{2,1,0:T(8,128)(2,1)} %bitcast.190), calls=%async_computation | async-start | bytes 3735552 | tf_op jit(solution)/shard_map/all_to_all | solution.py:163
  196.5 459.7 %reduce-scatter.10.cloned.1.call-start = ((), (), s32[]{:S(2)}) async-start(), calls=%async_computation.14 | async-start | bytes 20054016 | tf_op jit(solution)/shard_map/reduce_scatter | solution.py:114
  372.3 392.4 %reduce-scatter.12.cloned.1.call-start = ((), (), s32[]{:S(2)}) async-start(), calls=%async_computation.15 | async-start | bytes 20054016 | tf_op jit(solution)/shard_map/reduce_scatter | solution.py:117
  392.6 0.7 copy-start.28
  414.7 27.0 %all-to-all-start.1 = ((bf16[4,304,768]{2,0,1:T(4,128)(2,1)}), bf16[4,304,768]{2,0,1:T(4,128)(2,1)S(1)}, u32[]{:S(2)}, u32[]{:S(2)}) async-start(bf16[4,304,768]{2,0,1:T(4,128)(2,1)} %copy.81), calls=%async_computation.1 | async-start | bytes 3735552 | tf_op jit(solution)/shard_map/all_to_all | solution.py:165
  441.7 1.2 copy-start.11
  443.0 27.1 %all-to-all-start.3 = ((bf16[2,4,152,768]{3,2,1,0:T(8,128)(2,1)}), bf16[2,4,152,768]{3,2,1,0:T(8,128)(2,1)}, u32[]{:S(2)}, u32[]{:S(2)}) async-start(bf16[2,4,152,768]{3,2,1,0:T(8,128)(2,1)} %pad_maximum_fusion.1), calls=%async_computation.3 | async-start | bytes 3735552 | tf_op jit(solution)/shard_map/all_to_all | solution.py:195
  447.7 421.6 %reduce-scatter.8.cloned.1.call-start = ((), (), s32[]{:S(2)}) async-start(), calls=%async_computation.13 | async-start | bytes 2433024 | tf_op jit(solution)/shard_map/reduce_scatter | solution.py:229
  459.0 7.1 copy-start.22
  459.0 11.1 %copy-start.16 = (bf16[576,1216]{1,0:T(8,128)(2,1)S(1)}, bf16[576,1216]{1,0:T(8,128)(2,1)}, u32[]{:S(2)}) copy-start(bf16[576,1216]{1,0:T(8,128)(2,1)} %get-tuple-element.147) | copy-start | bytes 4202500
  470.1 3.0 copy-start.1
  473.1 1.2 copy-start.20
  474.2 1.9 copy-start.35
  474.9 1.2 copy-start.3
  483.7 510.5 %reduce-scatter.6.cloned.1.call-start = ((), (), s32[]{:S(2)}) async-start(), calls=%async_computation.12 | async-start | bytes 7299072 | tf_op jit(solution)/shard_map/reduce_scatter | solution.py:228
  584.3 1.8 copy-start.17
  584.3 2.4 copy-start.18
  586.7 2.2 copy-start.9
  586.7 2.2 copy-start.26
  586.7 2.2 copy-start.30
  586.7 2.2 copy-start.32
  587.2 1.7 copy-start.13
  594.7 1.3 copy-start.7
  596.2 53.8 %copy-start.10 = (bf16[576,768]{1,0:T(8,128)(2,1)S(1)}, bf16[576,768]{1,0:T(8,128)(2,1)}, u32[]{:S(2)}) copy-start(bf16[576,768]{1,0:T(8,128)(2,1)} %param.15) | copy-start | bytes 2654212
  650.0 4.0 copy-start.2
  650.0 4.0 copy-start.15
Sparse Core Ops, SparseCore 0:
  10.9 62.6 all-gather.5
  76.6 52.8 all-gather.7
  131.0 97.7 all-gather.11
  230.2 98.8 all-gather.9
  372.4 194.0 reduce-scatter.9
  570.5 194.1 reduce-scatter.11
  770.6 98.6 reduce-scatter.7
  875.5 118.6 reduce-scatter.5
